TPU v7x, 256 devices: a whole 4x4x8 slice. The times are simulated.
256 devices in a mesh: dp: 8 (over z), seq: 32 (over y, x, core).
Axes of the slice: x: 4, y: 4, z: 8, core: 2. Of those that a mesh axis runs over, the one named last changes fastest.
Arguments:
- latents: bfloat16 [16, 16384, 1152], P('dp', 'seq'), may hold values from -56 to 56
- out_grad: bfloat16 [16, 16384, 1152], P('dp', 'seq'), may hold values from -6 to 6
- phrases: bfloat16 [16, 32, 1152], P('dp'), may hold values from -6 to 6
- query_weight: bfloat16 [1152, 1152], replicated, may hold values from -0.1875 to 0.1875
- key_weight: bfloat16 [1152, 1152], P('seq'), may hold values from -0.1875 to 0.1875
- value_weight: bfloat16 [1152, 1152], P('seq'), may hold values from -0.1875 to 0.1875
- first_weight: bfloat16 [1152, 1152], P('seq'), may hold values from -0.1875 to 0.1875
- second_weight: bfloat16 [1152, 1152], P('seq'), may hold values from -0.1875 to 0.1875
- region_first: int32 [16, 32], P('dp'), may hold values from 0 to 127, as said below
- region_last: int32 [16, 32], P('dp'), may hold values from 0 to 127
- phrase_counts: int32 [16], P('dp'), may hold values from 8 to 32, as said below
Outputs:
- latent_grad: bfloat16 [16, 16384, 1152], P('dp', 'seq')
- phrase_grad: bfloat16 [16, 32, 1152], P('dp')
- first_grad: float32 [1152, 1152], P('seq')
- second_grad: float32 [1152, 1152], P('seq')
Inputs may be any that keep to these rules, and one draw needn't show every extreme that they name: region_first <= region_last for every phrase; phrase 0 of every image covers all 128 blocks. Slots from phrase_counts on are padding.
All inputs are finite; a program needn't handle non-finite values.
Results may differ from a plain program's by a relative error of at most 0.015.
The roundings to bfloat16 on the way count: a program that leaves them out, or rounds other values in their place, can miss the bound.
Values may be sent and summed in bfloat16 or wider, within the bound.
A program may use at most 128 MiB of HBM per device.

v0:
```python
import jax
import jax.numpy as jnp
from jax import lax
from jax.sharding import PartitionSpec as P

H = 16


def silu_slope(pre_act):
    sigmoid = jax.nn.sigmoid(pre_act)
    return sigmoid * (1.0 + pre_act * (1.0 - sigmoid))


def times_transposed(left_arg, right_arg):
    return lax.dot_general(
        left_arg, right_arg, (((1,), (1,)), ((), ())), preferred_element_type=jnp.float32
    )


def transposed_times(left_arg, right_arg):
    return lax.dot_general(
        left_arg, right_arg, (((0,), (0,)), ((), ())), preferred_element_type=jnp.float32
    )


def attention_grads(
    latents,
    out_grad,
    query_weight,
    key_rows,
    value_rows,
    region_first,
    region_last,
    phrase_counts,
    offset,
):
    images, tokens, features = latents.shape
    slot_count = key_rows.shape[1]
    head_count = H
    head_size = features // head_count
    score_scale = head_size ** (-0.5)
    queries = jnp.dot(
        latents.reshape(images * tokens, features), query_weight, preferred_element_type=jnp.float32
    ).astype(jnp.bfloat16)
    query_heads = queries.reshape(images, tokens, head_count, head_size)
    key_heads = key_rows.reshape(images, slot_count, head_count, head_size)
    value_heads = value_rows.reshape(images, slot_count, head_count, head_size)
    grad_heads = out_grad.reshape(images, tokens, head_count, head_size)
    scores = (
        jnp.einsum("ithd,iphd->ithp", query_heads, key_heads, preferred_element_type=jnp.float32)
        * score_scale
    )
    block_ids = (offset + jnp.arange(tokens, dtype=jnp.int32)) // (tokens // 4)
    phrase_ids = jnp.arange(slot_count, dtype=jnp.int32)
    visible = (
        (phrase_ids[None, None, :] < phrase_counts[:, None, None])
        & (region_first[:, None, :] <= block_ids[None, :, None])
        & (block_ids[None, :, None] <= region_last[:, None, :])
    )
    scores = jnp.where(visible[:, :, None, :], scores, -jnp.inf)
    row_max = jnp.max(scores, axis=-1, keepdims=True)
    exponent = jnp.exp(scores - row_max)
    attn_probs = exponent / jnp.sum(exponent, axis=-1, keepdims=True)
    probs_low = attn_probs.astype(jnp.bfloat16)
    prob_grad = jnp.einsum(
        "ithd,iphd->ithp", grad_heads, value_heads, preferred_element_type=jnp.float32
    )
    inner_sum = jnp.sum(attn_probs * prob_grad, axis=-1, keepdims=True)
    score_grad = (attn_probs * (prob_grad - inner_sum) * score_scale).astype(jnp.bfloat16)
    query_grad = jnp.einsum(
        "ithp,iphd->ithd", score_grad, key_heads, preferred_element_type=jnp.float32
    ).astype(jnp.bfloat16)
    latent_grad = times_transposed(
        query_grad.reshape(images * tokens, features), query_weight
    ).astype(jnp.bfloat16)
    key_part = jnp.einsum(
        "ithp,ithd->iphd", score_grad, query_heads, preferred_element_type=jnp.float32
    ).reshape(images, slot_count, features)
    value_part = jnp.einsum(
        "ithp,ithd->iphd", probs_low, grad_heads, preferred_element_type=jnp.float32
    ).reshape(images, slot_count, features)
    return (latent_grad.reshape(images, tokens, features), key_part, value_part)


def local(
    latents,
    out_grad,
    phrases,
    query_weight,
    key_weight,
    value_weight,
    first_weight,
    second_weight,
    region_first,
    region_last,
    phrase_counts,
):
    images, tokens, features = latents.shape
    slot_count = phrases.shape[1]
    shard_rows = first_weight.shape[0]
    col_start = lax.axis_index("seq") * shard_rows
    phrase_rows = phrases.reshape(images * slot_count, features)

    def own_cols(matrix):
        return lax.dynamic_slice_in_dim(matrix, col_start, shard_rows, 1)

    full_first, full_second, full_key, full_value = (
        lax.all_gather(first_weight, "seq", axis=0, tiled=True),
        lax.all_gather(second_weight, "seq", axis=0, tiled=True),
        lax.all_gather(key_weight, "seq", axis=0, tiled=True),
        lax.all_gather(value_weight, "seq", axis=0, tiled=True),
    )
    pre_act = jnp.dot(phrase_rows, full_first, preferred_element_type=jnp.float32)
    hidden = jax.nn.silu(pre_act).astype(jnp.bfloat16)
    encoded = jnp.dot(hidden, full_second, preferred_element_type=jnp.float32).astype(jnp.bfloat16)
    key_rows = jnp.dot(encoded, full_key, preferred_element_type=jnp.float32).astype(jnp.bfloat16)
    value_rows = jnp.dot(encoded, full_value, preferred_element_type=jnp.float32).astype(
        jnp.bfloat16
    )
    offset = lax.axis_index("seq") * tokens
    latent_grad, key_part, value_part = attention_grads(
        latents,
        out_grad,
        query_weight,
        key_rows.reshape(images, slot_count, features),
        value_rows.reshape(images, slot_count, features),
        region_first,
        region_last,
        phrase_counts,
        offset,
    )
    key_sum_grad, value_sum_grad = lax.psum((key_part, value_part), "seq")
    key_grad = key_sum_grad.astype(jnp.bfloat16).reshape(images * slot_count, features)
    value_grad = value_sum_grad.astype(jnp.bfloat16).reshape(images * slot_count, features)
    encoded_grad = (
        times_transposed(key_grad, full_key) + times_transposed(value_grad, full_value)
    ).astype(jnp.bfloat16)
    second_grad = transposed_times(own_cols(hidden), encoded_grad)
    hidden_grad = times_transposed(encoded_grad, full_second)
    act_grad = (hidden_grad * silu_slope(pre_act)).astype(jnp.bfloat16)
    first_grad = transposed_times(own_cols(phrase_rows), act_grad)
    phrase_grad = times_transposed(act_grad, full_first).astype(jnp.bfloat16)
    first_grad, second_grad = lax.psum((first_grad, second_grad), "dp")
    return (latent_grad, phrase_grad.reshape(images, slot_count, features), first_grad, second_grad)


def solution(mesh):
    in_specs = (
        P("dp", "seq", None),
        P("dp", "seq", None),
        P("dp", None, None),
        P(),
        P("seq", None),
        P("seq", None),
        P("seq", None),
        P("seq", None),
        P("dp", None),
        P("dp", None),
        P("dp"),
    )
    out_specs = (P("dp", "seq", None), P("dp", None, None), P("seq", None), P("seq", None))
    return jax.shard_map(local, mesh=mesh, in_specs=in_specs, out_specs=out_specs, check_vma=False)
```

profile of v0, /device:TPU:2, one launch (start us, length us, event | category | flops | bytes accessed | tf_op | source)
XLA Modules:
  0.0 481.6 jit_solution(8142799292820077217)
XLA Ops:
  7.2 0.7 all-gather.9.cloned.1.call-update
  8.0 0.7 all-gather.11.cloned.1.call-update
  8.7 0.7 all-gather.13.cloned.1.call-update
  9.4 0.5 all-gather.15.cloned.1.call-update
  10.0 0.0 all-reduce.5.cloned.1.call-start
  10.0 6.6 %convolution_convert_fusion.1 = bf16[1024,1152]{1,0:T(8,128)(2,1)} fusion(bf16[1024,1152]{1,0:T(8,128)(2,1)} %bitcast.91, bf16[1152,1152]{1,0:T(8,128)(2,1)S(1)} %copy-done), kind=kOutput, calls=%fused_computation.3 | convolution fusion | flops 2719088640 | bytes 7372800 | tf_op jit(solution)/shard_map/dot_general | solution.py:42
  16.6 9.6 %reshape.109 = bf16[2,512,16,72]{3,2,1,0:T(8,128)(2,1)} reshape(bf16[1024,1152]{1,0:T(8,128)(2,1)} %convolution_convert_fusion.1) | data formatting | bytes 4718592 | tf_op jit(solution)/shard_map/reshape | solution.py:45
  26.2 7.2 %copy.34 = bf16[2,512,16,72]{1,3,2,0:T(8,128)(2,1)} copy(bf16[2,512,16,72]{3,2,1,0:T(8,128)(2,1)} %reshape.109) | data formatting | bytes 4718592 | tf_op jit(solution)/shard_map/reshape | solution.py:45
  33.3 4.3 copy.35
  37.7 0.1 iota_compare_fusion
  37.8 0.1 compare_and_fusion
  37.9 25.3 %all-gather.9.cloned.1.call-done = bf16[32,36,1152]{2,1,0:T(8,128)(2,1)} async-done(((bf16[1,36,1152]{2,1,0:T(8,128)(2,1)}), bf16[32,36,1152]{2,1,0:T(8,128)(2,1)}) %all-gather.9.cloned.1.call-update) | async-done | bytes 2654224 | tf_op jit(solution)/shard_map/all_gather | solution.py:108
  63.1 5.2 %reshape.102 = bf16[1152,1152]{1,0:T(8,128)(2,1)} reshape(bf16[32,36,1152]{2,1,0:T(8,128)(2,1)} %all-gather.9.cloned.1.call-done) | data formatting | bytes 5308416
  68.3 47.0 %all-gather.11.cloned.1.call-done = bf16[32,36,1152]{2,1,0:T(8,128)(2,1)} async-done(((bf16[1,36,1152]{2,1,0:T(8,128)(2,1)}), bf16[32,36,1152]{2,1,0:T(8,128)(2,1)}) %all-gather.11.cloned.1.call-update) | async-done | bytes 2654224 | tf_op jit(solution)/shard_map/all_gather | solution.py:109
  115.3 5.1 %reshape.104 = bf16[1152,1152]{1,0:T(8,128)(2,1)} reshape(bf16[32,36,1152]{2,1,0:T(8,128)(2,1)} %all-gather.11.cloned.1.call-done) | data formatting | bytes 5308416
  120.4 47.0 %all-gather.13.cloned.1.call-done = bf16[32,36,1152]{2,1,0:T(8,128)(2,1)} async-done(((bf16[1,36,1152]{2,1,0:T(8,128)(2,1)}), bf16[32,36,1152]{2,1,0:T(8,128)(2,1)}) %all-gather.13.cloned.1.call-update) | async-done | bytes 2654224 | tf_op jit(solution)/shard_map/all_gather | solution.py:110
  167.4 5.1 %reshape.106 = bf16[1152,1152]{1,0:T(8,128)(2,1)} reshape(bf16[32,36,1152]{2,1,0:T(8,128)(2,1)} %all-gather.13.cloned.1.call-done) | data formatting | bytes 5308416
  172.6 3.2 multiply_convert_fusion
  175.8 0.6 convolution_convert_fusion.5
  176.4 0.1 copy-done.6
  176.4 0.6 convolution_convert_fusion.4
  177.0 0.5 reshape_reshape.6
  177.5 41.9 %all-gather.15.cloned.1.call-done = bf16[32,36,1152]{2,1,0:T(8,128)(2,1)} async-done(((bf16[1,36,1152]{2,1,0:T(8,128)(2,1)}), bf16[32,36,1152]{2,1,0:T(8,128)(2,1)}) %all-gather.15.cloned.1.call-update) | async-done | bytes 2654224 | tf_op jit(solution)/shard_map/all_gather | solution.py:111
  219.4 5.2 %reshape.108 = bf16[1152,1152]{1,0:T(8,128)(2,1)} reshape(bf16[32,36,1152]{2,1,0:T(8,128)(2,1)} %all-gather.15.cloned.1.call-done) | data formatting | bytes 5308416
  224.6 2.3 convolution_convert_fusion.3
  226.9 0.5 reshape_reshape.7
  227.4 3.5 fusion.13
  230.9 4.0 fusion.33
  234.9 3.8 convolution_bitcast_fusion
  238.7 5.8 %convolution_bitcast_fusion.1 = f32[2,32,16,72]{3,1,2,0:T(8,128)} fusion(bf16[2,512,16,72]{1,3,2,0:T(8,128)(2,1)} %copy.34, f32[2,16,32,512]{3,2,1,0:T(8,128)} %fusion.13, f32[2,512,16,32]{1,3,2,0:T(8,128)} %get-tuple-element.11, f32[2,512,16]{1,2,0:T(8,128)S(1)} %get-tuple-element.10), kind=kOutput, calls=%fused_computation.22 | convolution fusion | flops 79183904 | bytes 6914048 | tf_op jit(solution)/shard_map/ithp,ithd->iphd/dot_general | solution.py:76
  244.6 5.9 %convert_bitcast_fusion = bf16[2,512,16,72]{1,3,2,0:T(8,128)(2,1)} fusion(f32[2,16,32,512]{3,2,1,0:T(8,128)} %fusion.13, bf16[2,32,16,72]{3,2,1,0:T(8,128)(2,1)S(1)} %reshape_reshape.6, f32[2,512,16,32]{1,3,2,0:T(8,128)} %get-tuple-element.11, f32[2,512,16]{1,2,0:T(8,128)S(1)} %get-tuple-element.10), kind=kOutput, calls=%fused_computation.6 | convolution fusion | flops 80363552 | bytes 6766592 | tf_op jit(solution)/shard_map/ithp,iphd->ithd/dot_general | solution.py:70
  250.5 1.3 copy.40
  251.9 0.3 reshape.96
  252.1 1.3 copy.41
  253.5 1.0 reshape.98
  254.4 128.2 %all-reduce.6 = (bf16[2,32,1152]{2,1,0:T(8,128)(2,1)S(1)}, bf16[2,32,1152]{2,1,0:T(8,128)(2,1)S(1)}) all-reduce(f32[2,32,1152]{2,1,0:T(8,128)S(1)} %reshape.96, f32[2,32,1152]{2,1,0:T(8,128)} %reshape.98), channel_id=1, replica_groups=mesh['dp'=8,'seq'=32] {'seq'}, use_global_device_ids=true, to_apply=%region_3.4 | all-reduce | flops 147456 | bytes 884736 | tf_op jit(solution)/shard_map/psum | solution.py:132
  382.6 2.8 fusion.38
  385.5 0.9 fusion.2
  386.4 1.7 fusion.18
  388.2 0.9 fusion.3
  389.1 1.7 fusion.20
  390.8 4.1 copy.38
  394.9 2.1 copy.44
  397.0 6.8 %convolution_convert_fusion = bf16[1024,1152]{1,0:T(8,128)(2,1)} fusion(bf16[1024,1152]{0,1:T(8,128)(2,1)} %bitcast.81, bf16[1152,1152]{1,0:T(8,128)(2,1)S(1)} %copy-done), kind=kOutput, calls=%fused_computation.2 | convolution fusion | flops 2719088640 | bytes 7372800 | tf_op jit(solution)/shard_map/dot_general | solution.py:15
  403.8 1.6 convolution_convert_fusion.2
  405.4 66.5 %all-reduce.5.cloned.1.call-done = (f32[36,1152]{1,0:T(8,128)}, f32[36,1152]{1,0:T(8,128)}) async-done(((f32[36,1152]{1,0:T(8,128)}, f32[36,1152]{1,0:T(8,128)}), (f32[36,1152]{1,0:T(8,128)}, f32[36,1152]{1,0:T(8,128)})) %all-reduce.5.cloned.1.call-update) | async-done | bytes 331792 | tf_op jit(solution)/shard_map/psum | solution.py:143
  471.8 1.6 copy.61
  473.5 1.6 copy.62
  (29 shorter events, 0.2 us)
Async XLA Ops:
  7.2 2.9 copy-start
  7.2 56.0 %all-gather.9.cloned.1.call-start = ((), (), s32[]{:S(2)}) async-start(), calls=%async_computation | async-start | bytes 3041280 | tf_op jit(solution)/shard_map/all_gather | solution.py:108
  7.9 107.3 %all-gather.11.cloned.1.call-start = ((), (), s32[]{:S(2)}) async-start(), calls=%async_computation.1 | async-start | bytes 3041280 | tf_op jit(solution)/shard_map/all_gather | solution.py:109
  8.7 158.7 %all-gather.13.cloned.1.call-start = ((), (), s32[]{:S(2)}) async-start(), calls=%async_computation.2 | async-start | bytes 3041280 | tf_op jit(solution)/shard_map/all_gather | solution.py:110
  9.4 210.0 %all-gather.15.cloned.1.call-start = ((), (), s32[]{:S(2)}) async-start(), calls=%async_computation.3 | async-start | bytes 3041280 | tf_op jit(solution)/shard_map/all_gather | solution.py:111
  10.0 461.9 %all-reduce.5.cloned.1.call-start = ((), (), s32[]{:S(2)}) async-start(), calls=%async_computation.4 | async-start | bytes 737280 | tf_op jit(solution)/shard_map/psum | solution.py:143
  33.3 4.3 copy-start.11
  33.3 4.4 copy-start.9
  33.3 4.4 copy-start.10
  120.4 52.1 %copy-start.8 = (bf16[2,32,1152]{2,1,0:T(8,128)(2,1)S(1)}, bf16[2,32,1152]{2,1,0:T(8,128)(2,1)}, u32[]{:S(2)}) copy-start(bf16[2,32,1152]{2,1,0:T(8,128)(2,1)} %param.13) | copy-start | bytes 442372
  172.5 3.2 copy-start.4
  172.5 3.9 copy-start.3
  175.8 0.7 copy-start.6
  382.6 2.9 copy-start.2
  385.5 2.7 copy-start.5
  385.5 2.7 copy-start.7
  397.0 6.8 %copy-start.1 = (bf16[1152,1152]{1,0:T(8,128)(2,1)S(1)}, bf16[1152,1152]{1,0:T(8,128)(2,1)}, u32[]{:S(2)}) copy-start(bf16[1152,1152]{1,0:T(8,128)(2,1)} %reshape.102) | copy-start | bytes 7962628
Sparse Core Ops, SparseCore 0:
  10.6 52.4 all-gather.8
  65.8 49.4 all-gather.10
  117.9 49.4 all-gather.12
  169.9 49.4 all-gather.14
  397.1 74.6 all-reduce.4
where the time goes:
time: 483 us; the launch traced here: 482 us
  waiting for transfers between devices  230 us (48%)
  blocking collectives  128 us (27%)
  local copies, waits for them, and re-layouts  56.1 us (12%)
  matrix products  52.9 us (11%)
  between operations  13.9 us (3%)
    psum x1, blocking collectives, local(): key_sum_grad, value_sum_grad = lax.psum((key_part, value_part), 'seq')  128 us
    psum x1, waiting for transfers between devices, local(): first_grad, second_grad = lax.psum((first_grad, second_grad), 'dp')  66.5 us
    all_gather x1, waiting for transfers between devices, local(): lax.all_gather(key_weight, 'seq', axis=0, tiled=True)  47 us
    all_gather x1, waiting for transfers between devices, local(): lax.all_gather(second_weight, 'seq', axis=0, tiled=True)  47 us
    all_gather x1, waiting for transfers between devices, local(): lax.all_gather(value_weight, 'seq', axis=0, tiled=True)  41.9 us
    unnamed x32, local copies, waits for them, and re-layouts  30.4 us
    all_gather x1, waiting for transfers between devices, local(): lax.all_gather(first_weight, 'seq', axis=0, tiled=True)  25.3 us
    reshape x2, local copies, waits for them, and re-layouts, attention_grads(): query_heads = queries.reshape(images, tokens, head_count, head_size)  16.7 us
  transfers between devices with their start and end apart: 5, of which 5 were waited for; matrix products, arithmetic and copies ran while one was open for 12% of the time, Pallas kernels for 0%

commit v1 on v0

--- a/solution.py
+++ b/solution.py
@@ -107,7 +107,9 @@
     full_first, full_second, full_key, full_value = (
         lax.all_gather(first_weight, "seq", axis=0, tiled=True),
         lax.all_gather(second_weight, "seq", axis=0, tiled=True),
-        lax.all_gather(key_weight, "seq", axis=0, tiled=True),
+        jnp.concatenate(
+            lax.all_to_all(jnp.stack([key_weight] * lax.axis_size("seq")), "seq", 0, 0), axis=0
+        ),
         lax.all_gather(value_weight, "seq", axis=0, tiled=True),
     )
     pre_act = jnp.dot(phrase_rows, full_first, preferred_element_type=jnp.float32)

time: 483 us -> 450 us (0.932)
  waiting for transfers between devices: 230 us -> 187 us
  starting transfers between devices: 0.19 us -> 7.82 us
    all_gather x1 -> x0, waiting for transfers between devices: 47 us -> none  [local(): lax.all_gather(key_weight, 'seq', axis=0, tiled=True)]
    all_to_all x0 -> x1, waiting for transfers between devices: none -> 10.6 us  [local(): lax.all_to_all(jnp.stack([key_weight] * lax.axis_size('seq')), 'seq', 0, 0)]
    all_to_all x0 -> x1, starting transfers between devices: none -> 7.67 us  [local(): lax.all_to_all(jnp.stack([key_weight] * lax.axis_size('seq')), 'seq', 0, 0)]
    all_gather x1, waiting for transfers between devices: 25.3 us -> 19 us  [local(): lax.all_gather(first_weight, 'seq', axis=0, tiled=True)]
    reshape x0 -> x1, local copies, waits for them, and re-layouts: none -> 5.17 us  [local(): jnp.concatenate(lax.all_to_all(jnp.stack([key_weight] * lax.axis_size('se...]
    unnamed x32 -> x31, local copies, waits for them, and re-layouts: 30.4 us -> 25.2 us
  transfers between devices with their start and end apart: 5 -> 5, of which waited for: 5 -> 5; matrix products, arithmetic and copies ran while one was open for 12% -> 13% of each run, Pallas kernels for 0% -> 0%
where the time goes in v1:
time: 450 us; the launch traced here: 449 us
  waiting for transfers between devices  187 us (42%)
  blocking collectives  128 us (28%)
  local copies, waits for them, and re-layouts  58.8 us (13%)
  matrix products  52.7 us (12%)
  between operations  13.9 us (3%)
  starting transfers between devices  7.82 us (2%)
    psum x1, blocking collectives, local(): key_sum_grad, value_sum_grad = lax.psum((key_part, value_part), 'seq')  128 us
    psum x1, waiting for transfers between devices, local(): first_grad, second_grad = lax.psum((first_grad, second_grad), 'dp')  66.5 us
    all_gather x1, waiting for transfers between devices, local(): lax.all_gather(second_weight, 'seq', axis=0, tiled=True)  47 us
    all_gather x1, waiting for transfers between devices, local(): lax.all_gather(value_weight, 'seq', axis=0, tiled=True)  42.1 us
    unnamed x31, local copies, waits for them, and re-layouts  25.2 us
    all_gather x1, waiting for transfers between devices, local(): lax.all_gather(first_weight, 'seq', axis=0, tiled=True)  19 us
    reshape x2, local copies, waits for them, and re-layouts, attention_grads(): query_heads = queries.reshape(images, tokens, head_count, head_size)  16.7 us
    dot_general x5, matrix products, times_transposed(): lax.dot_general(left_arg, right_arg, (((1,), (1,)), ((), ())), preferred_...  13.1 us
  transfers between devices with their start and end apart: 5, of which 5 were waited for; matrix products, arithmetic and copies ran while one was open for 13% of the time, Pallas kernels for 0%

profile of v1, /device:TPU:2, one launch (start us, length us, event | category | flops | bytes accessed | tf_op | source)
XLA Modules:
  0.0 448.7 jit_solution(10623211661369061826)
XLA Ops:
  7.2 0.7 all-gather.7.cloned.1.call-update
  8.0 0.7 all-gather.9.cloned.1.call-update
  8.7 0.7 all-gather.11.cloned.1.call-update
  9.4 2.7 stack.2
  12.1 7.7 %all-to-all-start = ((bf16[32,36,1152]{2,1,0:T(8,128)(2,1)}), bf16[32,36,1152]{2,1,0:T(8,128)(2,1)}, u32[]{:S(2)}, u32[]{:S(2)}) async-start(bf16[32,36,1152]{2,1,0:T(8,128)(2,1)} %stack.2), calls=%async_computation | async-start | bytes 5898240 | tf_op jit(solution)/shard_map/all_to_all | solution.py:111
  19.8 6.6 %convolution_convert_fusion.1 = bf16[1024,1152]{1,0:T(8,128)(2,1)} fusion(bf16[1024,1152]{1,0:T(8,128)(2,1)} %bitcast.89, bf16[1152,1152]{1,0:T(8,128)(2,1)S(1)} %copy-done), kind=kOutput, calls=%fused_computation.3 | convolution fusion | flops 2719088640 | bytes 7372800 | tf_op jit(solution)/shard_map/dot_general | solution.py:42
  26.4 9.6 %reshape.113 = bf16[2,512,16,72]{3,2,1,0:T(8,128)(2,1)} reshape(bf16[1024,1152]{1,0:T(8,128)(2,1)} %convolution_convert_fusion.1) | data formatting | bytes 4718592 | tf_op jit(solution)/shard_map/reshape | solution.py:45
  36.0 7.1 %copy.34 = bf16[2,512,16,72]{1,3,2,0:T(8,128)(2,1)} copy(bf16[2,512,16,72]{3,2,1,0:T(8,128)(2,1)} %reshape.113) | data formatting | bytes 4718592 | tf_op jit(solution)/shard_map/reshape | solution.py:45
  43.1 4.3 copy.35
  47.5 0.1 iota_compare_fusion
  47.6 0.1 compare_and_fusion
  47.7 10.6 %all-to-all-done = bf16[32,36,1152]{2,1,0:T(8,128)(2,1)} async-done(((bf16[32,36,1152]{2,1,0:T(8,128)(2,1)}), bf16[32,36,1152]{2,1,0:T(8,128)(2,1)}, u32[]{:S(2)}, u32[]{:S(2)}) %all-to-all-start) | async-done | bytes 2654240 | tf_op jit(solution)/shard_map/all_to_all | solution.py:111
  58.2 5.2 %reshape.96 = bf16[1152,1152]{1,0:T(8,128)(2,1)} reshape(bf16[32,36,1152]{2,1,0:T(8,128)(2,1)} %all-to-all-done) | data formatting | bytes 5308416 | tf_op jit(solution)/shard_map/reshape | solution.py:110
  63.4 19.0 %all-gather.7.cloned.1.call-done = bf16[32,36,1152]{2,1,0:T(8,128)(2,1)} async-done(((bf16[1,36,1152]{2,1,0:T(8,128)(2,1)}), bf16[32,36,1152]{2,1,0:T(8,128)(2,1)}) %all-gather.7.cloned.1.call-update) | async-done | bytes 2654224 | tf_op jit(solution)/shard_map/all_gather | solution.py:108
  82.4 5.2 %reshape.108 = bf16[1152,1152]{1,0:T(8,128)(2,1)} reshape(bf16[32,36,1152]{2,1,0:T(8,128)(2,1)} %all-gather.7.cloned.1.call-done) | data formatting | bytes 5308416
  87.5 47.0 %all-gather.9.cloned.1.call-done = bf16[32,36,1152]{2,1,0:T(8,128)(2,1)} async-done(((bf16[1,36,1152]{2,1,0:T(8,128)(2,1)}), bf16[32,36,1152]{2,1,0:T(8,128)(2,1)}) %all-gather.9.cloned.1.call-update) | async-done | bytes 2654224 | tf_op jit(solution)/shard_map/all_gather | solution.py:109
  134.5 5.1 %reshape.110 = bf16[1152,1152]{1,0:T(8,128)(2,1)} reshape(bf16[32,36,1152]{2,1,0:T(8,128)(2,1)} %all-gather.9.cloned.1.call-done) | data formatting | bytes 5308416
  139.6 3.2 multiply_convert_fusion
  142.9 0.6 convolution_convert_fusion.5
  143.4 0.1 copy-done.6
  143.5 0.6 convolution_convert_fusion.4
  144.1 0.5 reshape_reshape.6
  144.6 42.1 %all-gather.11.cloned.1.call-done = bf16[32,36,1152]{2,1,0:T(8,128)(2,1)} async-done(((bf16[1,36,1152]{2,1,0:T(8,128)(2,1)}), bf16[32,36,1152]{2,1,0:T(8,128)(2,1)}) %all-gather.11.cloned.1.call-update) | async-done | bytes 2654224 | tf_op jit(solution)/shard_map/all_gather | solution.py:113
  186.6 5.2 %reshape.112 = bf16[1152,1152]{1,0:T(8,128)(2,1)} reshape(bf16[32,36,1152]{2,1,0:T(8,128)(2,1)} %all-gather.11.cloned.1.call-done) | data formatting | bytes 5308416
  191.8 2.3 convolution_convert_fusion.3
  194.2 0.5 reshape_reshape.7
  194.6 3.5 fusion.13
  198.1 3.9 fusion.33
  202.1 3.8 convolution_bitcast_fusion
  205.9 5.9 %convolution_bitcast_fusion.1 = f32[2,32,16,72]{3,1,2,0:T(8,128)} fusion(bf16[2,512,16,72]{1,3,2,0:T(8,128)(2,1)} %copy.34, f32[2,16,32,512]{3,2,1,0:T(8,128)} %fusion.13, f32[2,512,16,32]{1,3,2,0:T(8,128)} %get-tuple-element.11, f32[2,512,16]{1,2,0:T(8,128)S(1)} %get-tuple-element.10), kind=kOutput, calls=%fused_computation.22 | convolution fusion | flops 79183904 | bytes 6914048 | tf_op jit(solution)/shard_map/ithp,ithd->iphd/dot_general | solution.py:76
  211.8 5.8 %convert_bitcast_fusion = bf16[2,512,16,72]{1,3,2,0:T(8,128)(2,1)} fusion(f32[2,16,32,512]{3,2,1,0:T(8,128)} %fusion.13, bf16[2,32,16,72]{3,2,1,0:T(8,128)(2,1)S(1)} %reshape_reshape.6, f32[2,512,16,32]{1,3,2,0:T(8,128)} %get-tuple-element.11, f32[2,512,16]{1,2,0:T(8,128)S(1)} %get-tuple-element.10), kind=kOutput, calls=%fused_computation.6 | convolution fusion | flops 80363552 | bytes 6766592 | tf_op jit(solution)/shard_map/ithp,iphd->ithd/dot_general | solution.py:70
  217.6 1.3 copy.40
  218.9 0.3 reshape.102
  219.2 1.3 copy.41
  220.5 1.0 reshape.104
  221.5 128.2 %all-reduce.6 = (bf16[2,32,1152]{2,1,0:T(8,128)(2,1)S(1)}, bf16[2,32,1152]{2,1,0:T(8,128)(2,1)S(1)}) all-reduce(f32[2,32,1152]{2,1,0:T(8,128)S(1)} %reshape.102, f32[2,32,1152]{2,1,0:T(8,128)} %reshape.104), channel_id=1, replica_groups=mesh['dp'=8,'seq'=32] {'seq'}, use_global_device_ids=true, to_apply=%region_3.4 | all-reduce | flops 147456 | bytes 884736 | tf_op jit(solution)/shard_map/psum | solution.py:134
  349.7 2.8 fusion.38
  352.6 0.9 fusion.2
  353.5 1.7 fusion.18
  355.2 0.9 fusion.3
  356.2 1.7 fusion.20
  357.9 4.1 copy.38
  362.0 2.1 copy.44
  364.1 6.8 %convolution_convert_fusion = bf16[1024,1152]{1,0:T(8,128)(2,1)} fusion(bf16[1024,1152]{0,1:T(8,128)(2,1)} %bitcast.80, bf16[1152,1152]{1,0:T(8,128)(2,1)S(1)} %copy-done), kind=kOutput, calls=%fused_computation.2 | convolution fusion | flops 2719088640 | bytes 7372800 | tf_op jit(solution)/shard_map/dot_general | solution.py:15
  370.9 1.6 convolution_convert_fusion.2
  372.5 66.5 %all-reduce.5.cloned.1.call-done = (f32[36,1152]{1,0:T(8,128)}, f32[36,1152]{1,0:T(8,128)}) async-done(((f32[36,1152]{1,0:T(8,128)}, f32[36,1152]{1,0:T(8,128)}), (f32[36,1152]{1,0:T(8,128)}, f32[36,1152]{1,0:T(8,128)})) %all-reduce.5.cloned.1.call-update) | async-done | bytes 331792 | tf_op jit(solution)/shard_map/psum | solution.py:145
  438.9 1.6 copy.61
  440.6 1.6 copy.62
  (29 shorter events, 0.2 us)
Async XLA Ops:
  7.2 12.7 %copy-start = (bf16[1152,1152]{1,0:T(8,128)(2,1)S(1)}, bf16[1152,1152]{1,0:T(8,128)(2,1)}, u32[]{:S(2)}) copy-start(bf16[1152,1152]{1,0:T(8,128)(2,1)} %param.14) | copy-start | bytes 7962628
  7.2 75.2 %all-gather.7.cloned.1.call-start = ((), (), s32[]{:S(2)}) async-start(), calls=%async_computation.1 | async-start | bytes 3041280 | tf_op jit(solution)/shard_map/all_gather | solution.py:108
  7.9 126.6 %all-gather.9.cloned.1.call-start = ((), (), s32[]{:S(2)}) async-start(), calls=%async_computation.2 | async-start | bytes 3041280 | tf_op jit(solution)/shard_map/all_gather | solution.py:109
  8.7 178.0 %all-gather.11.cloned.1.call-start = ((), (), s32[]{:S(2)}) async-start(), calls=%async_computation.3 | async-start | bytes 3041280 | tf_op jit(solution)/shard_map/all_gather | solution.py:113
  12.1 46.1 %all-to-all-start = ((bf16[32,36,1152]{2,1,0:T(8,128)(2,1)}), bf16[32,36,1152]{2,1,0:T(8,128)(2,1)}, u32[]{:S(2)}, u32[]{:S(2)}) async-start(bf16[32,36,1152]{2,1,0:T(8,128)(2,1)} %stack.2), calls=%async_computation | async-start | bytes 5898240 | tf_op jit(solution)/shard_map/all_to_all | solution.py:111
  19.8 419.2 %all-reduce.5.cloned.1.call-start = ((), (), s32[]{:S(2)}) async-start(), calls=%async_computation.4 | async-start | bytes 737280 | tf_op jit(solution)/shard_map/psum | solution.py:145
  43.1 4.3 copy-start.11
  43.1 4.4 copy-start.9
  43.1 4.4 copy-start.10
  87.5 52.1 %copy-start.8 = (bf16[2,32,1152]{2,1,0:T(8,128)(2,1)S(1)}, bf16[2,32,1152]{2,1,0:T(8,128)(2,1)}, u32[]{:S(2)}) copy-start(bf16[2,32,1152]{2,1,0:T(8,128)(2,1)} %param.13) | copy-start | bytes 442372
  139.6 3.2 copy-start.4
  139.6 3.9 copy-start.3
  142.8 0.7 copy-start.6
  349.7 2.8 copy-start.2
  352.5 2.7 copy-start.5
  352.5 2.7 copy-start.7
  364.1 6.8 %copy-start.1 = (bf16[1152,1152]{1,0:T(8,128)(2,1)S(1)}, bf16[1152,1152]{1,0:T(8,128)(2,1)}, u32[]{:S(2)}) copy-start(bf16[1152,1152]{1,0:T(8,128)(2,1)} %reshape.108) | copy-start | bytes 7962628
Sparse Core Ops, SparseCore 0:
  10.6 71.6 all-gather.6
  85.0 49.4 all-gather.8
  137.1 49.4 all-gather.10
  364.2 74.6 all-reduce.4
